TPU v7x, 32 devices: a whole 2x2x4 slice. The times are simulated.
32 devices in a mesh: seq: 4 (over y, x), ctx: 4 (over z), fsdp: 2 (over core).
Axes of the slice: x: 2, y: 2, z: 4, core: 2. Of those that a mesh axis runs over, the one named last changes fastest.
Arguments:
- inputs: bfloat16 [8, 512, 2048], P(('seq', 'fsdp'), 'ctx'), may hold values from -6 to 6
- block_index: int32 [8, 4, 2], P(('seq', 'fsdp'), 'ctx'), may hold values from 0 to 7, as said below
- attention_gain: float32 [2048], replicated, may hold values from 0.1 to 1.9
- query_norm_gain: float32 [128], replicated, may hold values from 0.1 to 1.9
- key_gain: float32 [128], replicated, may hold values from 0.1 to 1.9
- feedforward_gain: float32 [2048], replicated, may hold values from 0.1 to 1.9
- attention_in: bfloat16 [2048, 4096], P(('seq', 'fsdp')), may hold values from -0.125 to 0.125
- attention_out: bfloat16 [2048, 2048], P(('seq', 'fsdp')), may hold values from -0.75 to 0.75
- gate_up: bfloat16 [2048, 12288], P(('seq', 'fsdp')), may hold values from -0.125 to 0.125
- down_weight: bfloat16 [2048, 6144], P(('seq', 'fsdp')), may hold values from -0.078125 to 0.078125
- grad_output: bfloat16 [8, 512, 2048], P(('seq', 'fsdp'), 'ctx'), may hold values from -6 to 6
Outputs:
- output: bfloat16 [8, 512, 2048], P(('seq', 'fsdp'), 'ctx')
- input_grad: bfloat16 [8, 512, 2048], P(('seq', 'fsdp'), 'ctx')
- attention_gain_grad: float32 [2048], replicated
- query_gain_grad: float32 [128], replicated
- key_gain_grad: float32 [128], replicated
- feedforward_gain_grad: float32 [2048], replicated
- attention_in_grad: float32 [2048, 4096], P(('seq', 'ctx', 'fsdp'))
- attention_out_grad: float32 [2048, 2048], P(('seq', 'ctx', 'fsdp'))
- gate_up_grad: float32 [2048, 12288], P(('seq', 'ctx', 'fsdp'))
- down_grad: float32 [2048, 6144], P(('seq', 'ctx', 'fsdp'))
Inputs may be any that keep to these rules, and one draw needn't show every extreme that they name: For each sequence s, block_index[s, c, 0] over c takes each of 0 to 3 once, and block_index[s, c, 1] = 7 - block_index[s, c, 0].
All inputs are finite; a program needn't handle non-finite values.
Results may differ from a plain program's by a relative error of at most 0.018.
Values may be sent and summed in bfloat16 or wider, within the bound.
No kernel may reach another device: no remote copies, remote signals or barrier semaphores. Data moves between devices by JAX's collectives and lax.ppermute only.
A program may use at most 832 MiB of HBM per device.

v0:
```python
import jax
import jax.numpy as jnp
from jax import lax
from jax.sharding import PartitionSpec as P

D = 2048
QUERY_HEADS = 16
KEY_VALUE_HEADS = 8
HEAD_SIZE = 128
FF = 6144
EPS = 1e-06
ROPE_BASE = 1000000.0
MASK_FLOOR = -1e30
PLANE = ("seq", "fsdp")
F32 = jnp.float32
BF16 = jnp.bfloat16


def rms_scale(values):
    return lax.rsqrt(jnp.mean(values * values, axis=-1, keepdims=True) + EPS)


def rms_back(grad_normed, normed_hat, scale, gain):
    grad_hat = grad_normed * gain
    inner = jnp.mean(grad_hat * normed_hat, axis=-1, keepdims=True)
    return scale * (grad_hat - normed_hat * inner)


def rope_tables(token_positions):
    half = HEAD_SIZE // 2
    rates = jnp.power(F32(ROPE_BASE), jnp.arange(half, dtype=F32) * (-2.0 / HEAD_SIZE))
    angles = token_positions.astype(F32)[:, None] * rates[None, :]
    angles = jnp.concatenate([angles, angles], axis=1)
    return (jnp.cos(angles), jnp.sin(angles))


def apply_rotation(values, cosine_table, sine_table):
    half = values.shape[-1] // 2
    turned = jnp.concatenate([-values[..., half:], values[..., :half]], axis=-1)
    return values * cosine_table[:, None, :] + turned * sine_table[:, None, :]


def rotate_back(grads, cosine_table, sine_table):
    half = grads.shape[-1] // 2
    scaled = grads * sine_table[:, None, :]
    turned = jnp.concatenate([scaled[..., half:], -scaled[..., :half]], axis=-1)
    return grads * cosine_table[:, None, :] + turned


def rows_by(left, right):
    return jnp.dot(left, right, preferred_element_type=F32)


def rows_by_t(left, right):
    return lax.dot_general(left, right, (((1,), (1,)), ((), ())), preferred_element_type=F32)


def t_by_rows(left, right):
    return lax.dot_general(left, right, (((0,), (0,)), ((), ())), preferred_element_type=F32)


def gather_ctx(rows):
    return lax.all_gather(rows, "ctx", axis=0, tiled=True)


def gather_plane(rows):
    return lax.all_gather(rows, PLANE, axis=0, tiled=True)


def scatter_ctx(partials):
    parts = lax.axis_size("ctx")
    pieces = lax.all_to_all(partials.astype(BF16), "ctx", 0, 0, tiled=True)
    pieces = pieces.reshape(parts, partials.shape[0] // parts, partials.shape[1])
    return jnp.sum(pieces.astype(F32), axis=0)


def scatter_weight(grad):
    seqs, ctxs, cores = (lax.axis_size("seq"), lax.axis_size("ctx"), lax.axis_size("fsdp"))
    rows = grad.shape[0] // (seqs * ctxs * cores)
    grad = grad.astype(BF16).reshape(seqs, ctxs, cores, rows, grad.shape[1])
    grad = jnp.transpose(grad, (0, 2, 1, 3, 4)).reshape(-1, grad.shape[-1])
    grad = lax.psum_scatter(grad, PLANE, scatter_dimension=0, tiled=True)
    grad = lax.all_to_all(grad, "ctx", 0, 0, tiled=True)
    return grad.reshape(ctxs, rows, grad.shape[-1])


def join_columns(pieces):
    parts, rows, width = pieces.shape
    return jnp.transpose(pieces, (1, 0, 2)).reshape(rows, parts * width).astype(F32)


def local(
    inputs,
    block_index,
    attention_gain,
    query_norm_gain,
    key_gain,
    feedforward_gain,
    attention_in,
    attention_out,
    gate_up,
    down_weight,
    grad_output,
):
    parts = lax.axis_size("ctx")
    me = lax.axis_index("ctx")
    tokens = inputs.shape[1]
    half_rows = tokens // 2
    length = tokens * parts
    query_heads = QUERY_HEADS // parts
    key_heads = max(1, KEY_VALUE_HEADS // parts)
    copies = key_heads * parts // KEY_VALUE_HEADS
    group = query_heads // key_heads
    query_width = query_heads * HEAD_SIZE
    key_width = key_heads * HEAD_SIZE
    all_query = QUERY_HEADS * HEAD_SIZE
    all_key = KEY_VALUE_HEADS * HEAD_SIZE
    hidden_width = FF // parts
    scale = HEAD_SIZE ** (-0.5)

    def columns(weight, start, width):
        return lax.dynamic_slice_in_dim(weight, start, width, axis=1)

    key_start = me // copies * key_width
    weight_in = gather_plane(
        jnp.concatenate(
            [
                columns(attention_in, me * query_width, query_width),
                columns(attention_in, all_query + key_start, key_width),
                columns(attention_in, all_query + all_key + key_start, key_width),
            ],
            axis=1,
        )
    )
    own_inputs = inputs[0]
    sequence_inputs = gather_ctx(own_inputs)
    blocks = lax.all_gather(block_index[0, 0], "ctx", axis=0, tiled=True)
    weight_out = gather_plane(attention_out)
    weight_gate_up = gather_plane(
        jnp.concatenate(
            [
                columns(gate_up, me * hidden_width, hidden_width),
                columns(gate_up, FF + me * hidden_width, hidden_width),
            ],
            axis=1,
        )
    )
    weight_down = gather_plane(columns(down_weight, me * hidden_width, hidden_width))
    own_grad = grad_output[0]
    sequence_grad = gather_ctx(own_grad)
    steps_along = jnp.arange(half_rows, dtype=jnp.int32)
    positions = (blocks[:, None] * half_rows + steps_along[None, :]).reshape(-1)
    cosine_table, sine_table = rope_tables(positions)
    rows = sequence_inputs.astype(F32)
    first_scale = rms_scale(rows)
    first_hat = rows * first_scale
    first_normed = (first_hat * attention_gain).astype(BF16)
    projected = rows_by(first_normed, weight_in)
    query = projected[:, :query_width].reshape(length, query_heads, HEAD_SIZE)
    key = projected[:, query_width : query_width + key_width].reshape(length, key_heads, HEAD_SIZE)
    value = projected[:, query_width + key_width :].astype(BF16)
    value = value.reshape(length, key_heads, HEAD_SIZE)
    query_scale = rms_scale(query)
    query_hat = query * query_scale
    key_scale = rms_scale(key)
    key_hat = key * key_scale
    rotary_query = (
        apply_rotation(query_hat * query_norm_gain, cosine_table, sine_table)
        .astype(BF16)
        .reshape(length, key_heads, group, HEAD_SIZE)
    )
    rotary_key = apply_rotation(key_hat * key_gain, cosine_table, sine_table).astype(BF16)
    scores = (
        jnp.einsum("qhgd,khd->hgqk", rotary_query, rotary_key, preferred_element_type=F32) * scale
    )
    allowed = positions[None, :] <= positions[:, None]
    scores = jnp.where(allowed, scores, MASK_FLOOR)
    peak = jnp.max(scores, axis=-1, keepdims=True)
    total = jnp.sum(jnp.where(allowed, jnp.exp(scores - peak), 0.0), axis=-1, keepdims=True)
    total_logarithm = peak + jnp.log(total)
    probs = jnp.where(allowed, jnp.exp(scores - total_logarithm), 0.0)
    weights = probs.astype(BF16)
    attended = jnp.einsum("hgqk,khd->qhgd", weights, value, preferred_element_type=F32)
    attended = attended.astype(BF16).reshape(length, query_width)
    own_attended = lax.all_to_all(attended, "ctx", 0, 1, tiled=True)
    own_rows = own_inputs.astype(F32)
    middle = own_rows + rows_by_t(own_attended, weight_out)
    second_scale = rms_scale(middle)
    second_hat = middle * second_scale
    second_normed = (second_hat * feedforward_gain).astype(BF16)
    sequence_second = gather_ctx(second_normed)
    grad_hidden = rows_by(sequence_grad, weight_down)
    gate_values = rows_by(sequence_second, weight_gate_up)
    gate = gate_values[:, :hidden_width]
    upward = gate_values[:, hidden_width:]
    sigmoid_gate = jax.nn.sigmoid(gate)
    silu_gate = gate * sigmoid_gate
    hidden = (silu_gate * upward).astype(BF16)
    grad_gate = grad_hidden * upward * sigmoid_gate * (1.0 + gate * (1.0 - sigmoid_gate))
    grad_upward = grad_hidden * silu_gate
    grad_gate_up = jnp.concatenate([grad_gate, grad_upward], axis=1).astype(BF16)
    grad_second = scatter_ctx(rows_by_t(grad_gate_up, weight_gate_up))
    down_pieces = scatter_weight(t_by_rows(sequence_grad, hidden))
    gate_up_pieces = scatter_weight(t_by_rows(sequence_second, grad_gate_up))
    output = middle + scatter_ctx(rows_by_t(hidden, weight_down))
    feedforward_part = jnp.sum(grad_second * second_hat, axis=0)
    grad_middle = own_grad.astype(F32) + rms_back(
        grad_second, second_hat, second_scale, feedforward_gain
    )
    grad_middle_short = grad_middle.astype(BF16)
    own_attended_grad = rows_by(grad_middle_short, weight_out).astype(BF16)
    attended_grad = lax.all_to_all(own_attended_grad, "ctx", 1, 0, tiled=True)
    sequence_middle_grad = gather_ctx(grad_middle_short)
    out_pieces = scatter_weight(t_by_rows(sequence_middle_grad, attended))
    delta = jnp.sum(
        (attended_grad.astype(F32) * attended.astype(F32)).reshape(
            length, key_heads, group, HEAD_SIZE
        ),
        axis=-1,
    )
    head_grads = attended_grad.reshape(length, key_heads, group, HEAD_SIZE)
    grad_probs = jnp.einsum("qhgd,khd->hgqk", head_grads, value, preferred_element_type=F32)
    grad_scores = (probs * (grad_probs - jnp.transpose(delta, (1, 2, 0))[..., None])).astype(BF16)
    grad_rotary_query = (
        jnp.einsum("hgqk,khd->qhgd", grad_scores, rotary_key, preferred_element_type=F32) * scale
    )
    grad_rotary_key = (
        jnp.einsum("hgqk,qhgd->khd", grad_scores, rotary_query, preferred_element_type=F32) * scale
    )
    value_grad = jnp.einsum("hgqk,qhgd->khd", weights, head_grads, preferred_element_type=F32)
    unrotated_query = rotate_back(
        grad_rotary_query.reshape(length, query_heads, HEAD_SIZE), cosine_table, sine_table
    )
    unrotated_key = rotate_back(grad_rotary_key, cosine_table, sine_table)
    query_part = jnp.sum(unrotated_query * query_hat, axis=(0, 1))
    key_part = jnp.sum(unrotated_key * key_hat, axis=(0, 1))
    grad_query = rms_back(unrotated_query, query_hat, query_scale, query_norm_gain)
    grad_key = rms_back(unrotated_key, key_hat, key_scale, key_gain)
    grad_projected = jnp.concatenate(
        [
            grad_query.reshape(length, query_width),
            grad_key.reshape(length, key_width),
            value_grad.reshape(length, key_width),
        ],
        axis=1,
    ).astype(BF16)
    partial_first = rows_by_t(grad_projected, weight_in)
    attention_part = jnp.sum(partial_first * first_hat, axis=0)
    grad_first = scatter_ctx(partial_first)
    in_pieces = scatter_weight(t_by_rows(first_normed, grad_projected))
    own_scale = rms_scale(own_rows)
    input_grad = grad_middle + rms_back(grad_first, own_rows * own_scale, own_scale, attention_gain)
    gain_sums = lax.psum(
        (attention_part, query_part, key_part, feedforward_part), ("seq", "ctx", "fsdp")
    )

    def merge_copies(pieces):
        shape = pieces.shape
        return jnp.sum(pieces.reshape(shape[0] // copies, copies, shape[1], shape[2]), axis=1)

    attention_in_grad = jnp.concatenate(
        [
            join_columns(in_pieces[:, :, :query_width]),
            join_columns(
                merge_copies(in_pieces[:, :, query_width : query_width + key_width].astype(F32))
            ),
            join_columns(merge_copies(in_pieces[:, :, query_width + key_width :].astype(F32))),
        ],
        axis=1,
    )
    gate_up_grad = jnp.concatenate(
        [
            join_columns(gate_up_pieces[:, :, :hidden_width]),
            join_columns(gate_up_pieces[:, :, hidden_width:]),
        ],
        axis=1,
    )
    return (
        output.astype(BF16)[None],
        input_grad.astype(BF16)[None],
        gain_sums[0],
        gain_sums[1],
        gain_sums[2],
        gain_sums[3],
        attention_in_grad,
        join_columns(out_pieces),
        gate_up_grad,
        join_columns(down_pieces),
    )


def solution(mesh):
    tokens = P(("seq", "fsdp"), "ctx", None)
    weight = P(("seq", "fsdp"), None)
    grad = P(("seq", "ctx", "fsdp"), None)
    in_specs = (tokens, tokens, P(), P(), P(), P(), weight, weight, weight, weight, tokens)
    out_specs = (tokens, tokens, P(), P(), P(), P(), grad, grad, grad, grad)
    return jax.shard_map(local, mesh=mesh, in_specs=in_specs, out_specs=out_specs, check_vma=False)
```

profile of v0, /device:TPU:0, one launch (start us, length us, event | category | flops | bytes accessed | tf_op | source)
XLA Modules:
  0.0 858.8 jit_solution(17743608366235928111)
XLA Ops:
  13.2 10.0 %all-reduce = s32[8]{0:T(128)S(1)} all-reduce(s32[8]{0:T(128)S(1)} %bitcast_dynamic-update-slice_fusion), channel_id=3, replica_groups=mesh['seq'=4,'ctx'=4,'fsdp'=2] {'ctx'}, use_global_device_ids=true, to_apply=%add | all-reduce | flops 8 | bytes 64
  25.5 32.6 %all-gather.24.cloned.1.call-done = bf16[1,512,2048]{2,1,0:T(8,128)(2,1)} async-done(((bf16[1,128,2048]{2,1,0:T(8,128)(2,1)}), bf16[1,512,2048]{2,1,0:T(8,128)(2,1)}) %all-gather.24.cloned.1.call-update) | async-done | bytes 2097168 | tf_op jit(solution)/shard_map/all_gather | solution.py:63
  60.1 35.7 %all-gather.12.cloned.1.call-done = bf16[2048,1024]{1,0:T(8,128)(2,1)} async-done(((bf16[256,1024]{1,0:T(8,128)(2,1)}), bf16[2048,1024]{1,0:T(8,128)(2,1)}) %all-gather.12.cloned.1.call-update) | async-done | bytes 4194320 | tf_op jit(solution)/shard_map/all_gather | solution.py:67
  95.8 5.2 fusion.29
  109.7 2.4 multiply_reduce_fusion.9
  113.1 2.5 copy.253
  128.9 19.6 %all_to_all.98 = bf16[4,128,512]{1,2,0:T(8,128)(2,1)} all-to-all(bf16[4,128,512]{1,2,0:T(8,128)(2,1)S(1)} %copy.204), channel_id=1, replica_groups=mesh['seq'=4,'ctx'=4,'fsdp'=2] {'ctx'}, dimensions={0} | all-to-all | bytes 1048576 | tf_op jit(solution)/shard_map/all_to_all | solution.py:185
  148.5 3.6 all-gather.14.cloned.1.call-done
  152.0 6.5 multiply_reduce_fusion.5
  165.1 41.2 %all-gather.16.cloned.1.call-done = bf16[512,2048]{1,0:T(8,128)(2,1)} async-done(((bf16[128,2048]{1,0:T(8,128)(2,1)}), bf16[512,2048]{1,0:T(8,128)(2,1)}) %all-gather.16.cloned.1.call-update) | async-done | bytes 2097168 | tf_op jit(solution)/shard_map/all_gather | solution.py:63
  206.3 73.1 %all-gather.18.cloned.1.call-done = bf16[2048,3072]{1,0:T(8,128)(2,1)} async-done(((bf16[256,3072]{1,0:T(8,128)(2,1)}), bf16[2048,3072]{1,0:T(8,128)(2,1)}) %all-gather.18.cloned.1.call-update) | async-done | bytes 12582928 | tf_op jit(solution)/shard_map/all_gather | solution.py:67
  279.5 11.9 %fusion.50 = f32[512,3072]{1,0:T(8,128)} fusion(bf16[512,2048]{1,0:T(8,128)(2,1)} %all-gather.16.cloned.1.call-done, bf16[2048,3072]{1,0:T(8,128)(2,1)} %all-gather.18.cloned.1.call-done), kind=kOutput, calls=%fused_computation.145 | convolution fusion | flops 6442450944 | bytes 20971520 | tf_op jit(solution)/shard_map/dot_general | solution.py:51
  291.4 35.2 %all-gather.26.cloned.1.call-done = bf16[1,512,2048]{2,1,0:T(8,128)(2,1)} async-done(((bf16[1,128,2048]{2,1,0:T(8,128)(2,1)}), bf16[1,512,2048]{2,1,0:T(8,128)(2,1)}) %all-gather.26.cloned.1.call-update) | async-done | bytes 2097168 | tf_op jit(solution)/shard_map/all_gather | solution.py:63
  326.6 46.7 %all-gather.20.cloned.1.call-done = bf16[2048,1536]{1,0:T(8,128)(2,1)} async-done(((bf16[256,1536]{1,0:T(8,128)(2,1)}), bf16[2048,1536]{1,0:T(8,128)(2,1)}) %all-gather.20.cloned.1.call-update) | async-done | bytes 6291472 | tf_op jit(solution)/shard_map/all_gather | solution.py:67
  373.3 10.9 %multiply_convert_fusion.1 = (bf16[512,1536]{1,0:T(8,128)(2,1)S(1)}, bf16[512,1536]{1,0:T(8,128)(2,1)S(1)}, bf16[512,1536]{1,0:T(8,128)(2,1)}) fusion(f32[512,3072]{1,0:T(8,128)} %fusion.50, bf16[2048,1536]{1,0:T(8,128)(2,1)} %all-gather.20.cloned.1.call-done, bf16[1,512,2048]{2,1,0:T(8,128)(2,1)} %all-gather.26.cloned.1.call-done), kind=kOutput, calls=%fused_computation.24 | convolution fusion | flops 3233021952 | bytes 19398656 | tf_op jit(solution)/shard_map/dot_general | solution.py:51
  384.2 6.9 convolution_convert_fusion.3
  391.1 53.1 %all_to_all.99 = bf16[4,128,2048]{2,1,0:T(8,128)(2,1)S(1)} all-to-all(bf16[4,128,2048]{2,1,0:T(8,128)(2,1)S(1)} %bitcast.232), channel_id=1, replica_groups=mesh['seq'=4,'ctx'=4,'fsdp'=2] {'ctx'}, dimensions={0} | all-to-all | bytes 4194304 | tf_op jit(solution)/shard_map/all_to_all | solution.py:72
  446.7 43.7 %all-gather.22.cloned.1.call-done = bf16[512,2048]{1,0:T(8,128)(2,1)} async-done(((bf16[128,2048]{1,0:T(8,128)(2,1)}), bf16[512,2048]{1,0:T(8,128)(2,1)}) %all-gather.22.cloned.1.call-update) | async-done | bytes 2097168 | tf_op jit(solution)/shard_map/all_gather | solution.py:63
  490.4 2.9 convolution_convert_fusion.4
  494.9 8.2 fusion
  503.1 8.7 %copy.233 = bf16[2048,1536]{1,0:T(8,128)(2,1)} copy(bf16[2048,1536]{0,1:T(8,128)(2,1)} %fusion) | data formatting | bytes 12582912 | tf_op jit(solution)/shard_map/convert_element_type | solution.py:80
  511.8 6.1 copy.234
  519.0 5.6 convolution_convert_fusion.6
  526.6 4.1 all-to-all-start.3
  534.3 11.1 %all-to-all-done.3 = bf16[128,4,512]{0,2,1:T(8,128)(2,1)} async-done(((bf16[128,4,512]{0,2,1:T(8,128)(2,1)}), bf16[128,4,512]{0,2,1:T(8,128)(2,1)}, u32[]{:S(2)}, u32[]{:S(2)}) %all-to-all-start.3) | async-done | bytes 524320 | tf_op jit(solution)/shard_map/all_to_all | solution.py:212
  547.2 5.2 fusion.15
  554.4 4.0 fusion.7
  563.0 3.1 broadcast_multiply_fusion.1
  578.6 2.6 copy.257
  587.0 2.7 convolution_convert_fusion.2
  589.7 2.4 copy.224
  592.2 9.2 %convolution_convert_fusion = bf16[2048,3072]{1,0:T(8,128)(2,1)S(1)} fusion(bf16[512,2048]{1,0:T(8,128)(2,1)} %all-gather.16.cloned.1.call-done, bf16[512,1536]{1,0:T(8,128)(2,1)} %copy-done.47, bf16[512,1536]{1,0:T(8,128)(2,1)} %copy-done.46), kind=kOutput, calls=%fused_computation | convolution fusion | flops 6455033856 | bytes 17825792 | tf_op jit(solution)/shard_map/dot_general | solution.py:59
  601.4 5.6 copy.230
  607.1 8.4 convolution_convert_fusion.5
  615.6 4.6 all-to-all-start.1
  620.2 6.6 fusion.4
  626.8 41.7 %all-to-all-done.1 = bf16[4,128,2048]{2,1,0:T(8,128)(2,1)} async-done(((bf16[4,128,2048]{2,1,0:T(8,128)(2,1)}), bf16[4,128,2048]{2,1,0:T(8,128)(2,1)}, u32[]{:S(2)}, u32[]{:S(2)}) %all-to-all-start.1) | async-done | bytes 2097184 | tf_op jit(solution)/shard_map/all_to_all | solution.py:72
  668.5 52.4 %all_to_all.100 = bf16[4,128,2048]{2,1,0:T(8,128)(2,1)} all-to-all(bf16[4,128,2048]{2,1,0:T(8,128)(2,1)} %bitcast.231), channel_id=1, replica_groups=mesh['seq'=4,'ctx'=4,'fsdp'=2] {'ctx'}, dimensions={0} | all-to-all | bytes 4194304 | tf_op jit(solution)/shard_map/all_to_all | solution.py:72
  720.9 3.4 all-to-all-start.6
  724.3 8.0 all-to-all-done.6
  732.3 4.2 all-to-all-start.8
  736.8 17.3 %all-to-all-done.8 = bf16[4,64,1536]{2,1,0:T(8,128)(2,1)} async-done(((bf16[4,64,1536]{2,1,0:T(8,128)(2,1)}), bf16[4,64,1536]{2,1,0:T(8,128)(2,1)}, u32[]{:S(2)}, u32[]{:S(2)}) %all-to-all-start.8) | async-done | bytes 786464 | tf_op jit(solution)/shard_map/all_to_all | solution.py:83
  754.1 4.1 all-to-all-start.5
  758.2 3.0 convert_reduce_fusion.2
  761.2 41.2 %all-reduce.1 = (f32[2048]{0:T(1024)}, f32[128]{0:T(128)}, f32[128]{0:T(128)}, f32[2048]{0:T(1024)}) all-reduce(f32[2048]{0:T(1024)S(1)} %get-tuple-element.26, f32[128]{0:T(128)S(1)} %get-tuple-element.10, f32[128]{0:T(128)S(1)} %get-tuple-element.14, ...), channel_id=1, replica_groups=mesh['seq'=4,'ctx'=4,'fsdp'=2] {'seq','ctx','fsdp'}, use_global_device_ids=true, to_apply=%region_16.17 | all-reduce | flops 4352 | bytes 34816 | tf_op jit(solution)/shard_map/psum | solution.py:253
  805.9 4.4 all-to-all-start.7
  810.3 3.0 fusion.32
  819.8 27.4 %all-to-all-done.7 = bf16[4,64,3072]{2,1,0:T(8,128)(2,1)} async-done(((bf16[4,64,3072]{2,1,0:T(8,128)(2,1)}), bf16[4,64,3072]{2,1,0:T(8,128)(2,1)}, u32[]{:S(2)}, u32[]{:S(2)}) %all-to-all-start.7) | async-done | bytes 1572896 | tf_op jit(solution)/shard_map/all_to_all | solution.py:83
  (222 shorter events, 90.6 us)
Async XLA Ops:
  7.2 156.9 %copy-start = (bf16[256,6144]{1,0:T(8,128)(2,1)S(1)}, bf16[256,6144]{1,0:T(8,128)(2,1)}, u32[]{:S(2)}) copy-start(bf16[256,6144]{1,0:T(8,128)(2,1)} %param.20) | copy-start | bytes 9437188
  7.2 4.6 copy-start.45
  7.2 5.9 copy-start.44
  7.2 50.8 %all-gather.24.cloned.1.call-start = ((), (), s32[]{:S(2)}) async-start(), calls=%async_computation.23 | async-start | bytes 2621440 | tf_op jit(solution)/shard_map/all_gather | solution.py:63
  8.0 87.9 %all-gather.12.cloned.1.call-start = ((), (), s32[]{:S(2)}) async-start(), calls=%async_computation.13 | async-start | bytes 4718592 | tf_op jit(solution)/shard_map/all_gather | solution.py:67
  10.1 85.7 %copy-start.40 = (f32[2048]{0:T(1024)S(1)}, f32[2048]{0:T(1024)}, u32[]{:S(2)}) copy-start(f32[2048]{0:T(1024)} %param.13) | copy-start | bytes 24580
  11.0 141.0 %all-gather.14.cloned.1.call-start = ((), (), s32[]{:S(2)}) async-start(), calls=%async_computation.14 | async-start | bytes 9437184 | tf_op jit(solution)/shard_map/all_gather | solution.py:67
  11.8 194.6 %all-gather.16.cloned.1.call-start = ((), (), s32[]{:S(2)}) async-start(), calls=%async_computation.15 | async-start | bytes 2621440 | tf_op jit(solution)/shard_map/all_gather | solution.py:63
  105.5 11.6 %copy-start.41 = (f32[128]{0:T(128)S(1)}, f32[128]{0:T(128)}, u32[]{:S(2)}) copy-start(f32[128]{0:T(128)} %param.15) | copy-start | bytes 1540
  113.1 6.7 copy-start.42
  117.1 2.8 copy-start.2
  122.4 3.2 copy-start.6
  152.0 7.5 copy-start.39
  160.5 118.9 %all-gather.18.cloned.1.call-start = ((), (), s32[]{:S(2)}) async-start(), calls=%async_computation.16 | async-start | bytes 14155776 | tf_op jit(solution)/shard_map/all_gather | solution.py:67
  163.4 163.1 %all-gather.26.cloned.1.call-start = ((), (), s32[]{:S(2)}) async-start(), calls=%async_computation.24 | async-start | bytes 2621440 | tf_op jit(solution)/shard_map/all_gather | solution.py:63
  164.0 209.3 %all-gather.20.cloned.1.call-start = ((), (), s32[]{:S(2)}) async-start(), calls=%async_computation.17 | async-start | bytes 7077888 | tf_op jit(solution)/shard_map/all_gather | solution.py:67
  165.0 325.4 %all-gather.22.cloned.1.call-start = ((), (), s32[]{:S(2)}) async-start(), calls=%async_computation.19 | async-start | bytes 2621440 | tf_op jit(solution)/shard_map/all_gather | solution.py:63
  373.3 10.9 %copy-start.43 = (bf16[2048,3072]{1,0:T(8,128)(2,1)S(1)}, bf16[2048,3072]{1,0:T(8,128)(2,1)}, u32[]{:S(2)}) copy-start(bf16[2048,3072]{1,0:T(8,128)(2,1)} %all-gather.18.cloned.1.call-done) | copy-start | bytes 37748740
  384.2 6.9 copy-start.46
  384.2 6.9 copy-start.47
  391.1 53.5 %copy-start.5 = (f32[128,2048]{1,0:T(8,128)S(1)}, f32[128,2048]{1,0:T(8,128)}, u32[]{:S(2)}) copy-start(f32[128,2048]{1,0:T(8,128)} %copy-done.4) | copy-start | bytes 3145732
  444.7 45.7 %copy-start.29 = (bf16[2,128,2,512]{3,1,2,0:T(8,128)(2,1)S(1)}, bf16[2,128,2,512]{3,1,2,0:T(8,128)(2,1)}, u32[]{:S(2)}) copy-start(bf16[2,128,2,512]{3,1,2,0:T(8,128)(2,1)} %convolution_convert_fusion.7) | copy-start | bytes 1572868
  446.5 274.4 %reduce-scatter.7.cloned.1.call-start = ((), (), s32[]{:S(2)}) async-start(), calls=%async_computation.20 | async-start | bytes 2359296 | tf_op jit(solution)/shard_map/reduce_scatter | solution.py:82
  494.9 229.4 %reduce-scatter.11.cloned.1.call-start = ((), (), s32[]{:S(2)}) async-start(), calls=%async_computation.22 | async-start | bytes 7077888 | tf_op jit(solution)/shard_map/reduce_scatter | solution.py:82
  519.0 12.2 %copy-start.22 = (f32[512,128]{0,1:T(8,128)S(1)}, f32[512,128]{0,1:T(8,128)}, u32[]{:S(2)}) copy-start(f32[512,128]{0,1:T(8,128)} %get-tuple-element.46) | copy-start | bytes 786436
  519.0 13.1 %copy-start.20 = (f32[512,128]{0,1:T(8,128)S(1)}, f32[512,128]{0,1:T(8,128)}, u32[]{:S(2)}) copy-start(f32[512,128]{0,1:T(8,128)} %get-tuple-element.47) | copy-start | bytes 786436
  526.6 18.8 %all-to-all-start.3 = ((bf16[128,4,512]{0,2,1:T(8,128)(2,1)}), bf16[128,4,512]{0,2,1:T(8,128)(2,1)}, u32[]{:S(2)}, u32[]{:S(2)}) async-start(bf16[128,4,512]{0,2,1:T(8,128)(2,1)} %bitcast.26), calls=%async_computation.3 | async-start | bytes 1048576 | tf_op jit(solution)/shard_map/all_to_all | solution.py:212
  530.8 206.0 %reduce-scatter.5.cloned.1.call-start = ((), (), s32[]{:S(2)}) async-start(), calls=%async_computation.18 | async-start | bytes 4718592 | tf_op jit(solution)/shard_map/reduce_scatter | solution.py:82
  547.2 7.0 copy-start.31
  547.2 7.0 copy-start.30
  554.3 4.1 copy-start.16
  554.4 4.1 copy-start.26
  569.0 6.8 copy-start.3
  578.6 6.5 copy-start.32
  581.2 4.1 copy-start.17
  581.2 4.1 copy-start.18
  581.2 4.1 copy-start.24
  592.1 213.7 %reduce-scatter.9.cloned.1.call-start = ((), (), s32[]{:S(2)}) async-start(), calls=%async_computation.21 | async-start | bytes 14155776 | tf_op jit(solution)/shard_map/reduce_scatter | solution.py:82
  615.6 4.6 copy-start.34
  615.6 4.6 copy-start.38
  615.6 52.9 %all-to-all-start.1 = ((bf16[4,128,2048]{2,1,0:T(8,128)(2,1)}), bf16[4,128,2048]{2,1,0:T(8,128)(2,1)}, u32[]{:S(2)}, u32[]{:S(2)}) async-start(bf16[4,128,2048]{2,1,0:T(8,128)(2,1)} %bitcast.230), calls=%async_computation.1 | async-start | bytes 4194304 | tf_op jit(solution)/shard_map/all_to_all | solution.py:72
  668.5 68.0 %copy-start.8 = (bf16[1,128,2048]{2,1,0:T(8,128)(2,1)S(1)}, bf16[1,128,2048]{2,1,0:T(8,128)(2,1)}, u32[]{:S(2)}) copy-start(bf16[1,128,2048]{2,1,0:T(8,128)(2,1)} %param.11) | copy-start | bytes 1572868
  720.9 11.5 %all-to-all-start.6 = ((bf16[4,64,512]{2,1,0:T(8,128)(2,1)}), bf16[4,64,512]{2,1,0:T(8,128)(2,1)S(1)}, u32[]{:S(2)}, u32[]{:S(2)}) async-start(bf16[4,64,512]{2,1,0:T(8,128)(2,1)} %bitcast.250), calls=%async_computation.8 | async-start | bytes 524288 | tf_op jit(solution)/shard_map/all_to_all | solution.py:83
  732.3 21.7 %all-to-all-start.8 = ((bf16[4,64,1536]{2,1,0:T(8,128)(2,1)}), bf16[4,64,1536]{2,1,0:T(8,128)(2,1)}, u32[]{:S(2)}, u32[]{:S(2)}) async-start(bf16[4,64,1536]{2,1,0:T(8,128)(2,1)} %bitcast.243), calls=%async_computation.12 | async-start | bytes 1572864 | tf_op jit(solution)/shard_map/all_to_all | solution.py:83
  754.1 51.8 %all-to-all-start.5 = ((bf16[4,64,1024]{2,1,0:T(8,128)(2,1)}), bf16[4,64,1024]{2,1,0:T(8,128)(2,1)}, u32[]{:S(2)}, u32[]{:S(2)}) async-start(bf16[4,64,1024]{2,1,0:T(8,128)(2,1)} %bitcast.246), calls=%async_computation.6 | async-start | bytes 1048576 | tf_op jit(solution)/shard_map/all_to_all | solution.py:83
  805.5 4.7 copy-start.14
  805.9 41.3 %all-to-all-start.7 = ((bf16[4,64,3072]{2,1,0:T(8,128)(2,1)}), bf16[4,64,3072]{2,1,0:T(8,128)(2,1)}, u32[]{:S(2)}, u32[]{:S(2)}) async-start(bf16[4,64,3072]{2,1,0:T(8,128)(2,1)} %bitcast.239), calls=%async_computation.10 | async-start | bytes 3145728 | tf_op jit(solution)/shard_map/all_to_all | solution.py:83
  848.7 3.0 copy-start.1
  (18 other events, 25.9 us)
Sparse Core Ops, SparseCore 0:
  9.6 48.4 all-gather.23
  60.5 35.2 all-gather.11
  97.7 54.2 all-gather.13
  160.6 45.6 all-gather.15
  208.6 70.7 all-gather.17
  280.9 45.6 all-gather.25
  329.0 44.1 all-gather.19
  446.6 43.7 all-gather.21
  495.0 39.9 reduce-scatter.6
  538.2 61.7 reduce-scatter.10
  603.4 51.1 reduce-scatter.4
  657.9 92.2 reduce-scatter.8
where the time goes:
time: 868 us; the launch traced here: 859 us
  waiting for transfers between devices  419 us (48%)
  blocking collectives  176 us (20%)
  matrix products  101 us (12%)
  local copies, waits for them, and re-layouts  79.5 us (9%)
  other arithmetic  40.4 us (5%)
  starting transfers between devices  25.9 us (3%)
  between operations  15.9 us (2%)
    all_gather x4, waiting for transfers between devices, gather_plane(): return lax.all_gather(rows, PLANE, axis=0, tiled=True)  159 us
    all_gather x4, waiting for transfers between devices, gather_ctx(): return lax.all_gather(rows, 'ctx', axis=0, tiled=True)  153 us
    all_to_all x2, blocking collectives, scatter_ctx(): pieces = lax.all_to_all(partials.astype(BF16), 'ctx', 0, 0, tiled=True)  106 us
    all_to_all x4, waiting for transfers between devices, scatter_weight(): grad = lax.all_to_all(grad, 'ctx', 0, 0, tiled=True)  52.7 us
    all_to_all x1, waiting for transfers between devices, scatter_ctx(): pieces = lax.all_to_all(partials.astype(BF16), 'ctx', 0, 0, tiled=True)  41.7 us
    psum x1, blocking collectives, local(): lax.psum((attention_part, query_part, key_part, feedforward_part), ('seq'...  41.2 us
    dot_general x4, matrix products, rows_by(): return jnp.dot(left, right, preferred_element_type=F32)  33.6 us
    dot_general x4, matrix products, rows_by_t(): lax.dot_general(left, right, (((1,), (1,)), ((), ())), preferred_element_...  28.5 us
  transfers between devices with their start and end apart: 18, of which 13 were waited for; matrix products, arithmetic and copies ran while one was open for 21% of the time, Pallas kernels for 0%

commit v1 on v0

--- a/solution.py
+++ b/solution.py
@@ -1,3 +1,4 @@
+import functools
 import jax
 import jax.numpy as jnp
 from jax import lax
@@ -16,6 +17,23 @@
 BF16 = jnp.bfloat16
 
 
+def raise_the_record(local_array, along_axis, pos_dim):
+    heard, y_new = (lax.axis_size(along_axis), lax.axis_index(along_axis))
+    high, even = (local_array, 1)
+    while even < heard:
+        mat_out = lax.ppermute(
+            high, along_axis, tuple(((tick, tick ^ even) for tick in range(heard)))
+        )
+        mid_arr = jnp.concatenate([high, mat_out], axis=pos_dim)
+        current_value = jnp.concatenate([mat_out, high], axis=pos_dim)
+        high = jnp.where(y_new & even == 0, mid_arr, current_value)
+        even = 2 * even
+    return high
+
+
+derive_sources_all = functools.partial(raise_the_record, along_axis="ctx", pos_dim=0)
+
+
 def rms_scale(values):
     return lax.rsqrt(jnp.mean(values * values, axis=-1, keepdims=True) + EPS)
 
@@ -60,7 +78,7 @@
 
 
 def gather_ctx(rows):
-    return lax.all_gather(rows, "ctx", axis=0, tiled=True)
+    return derive_sources_all(rows)
 
 
 def gather_plane(rows):

time: 868 us -> 731 us (0.84)
  waiting for transfers between devices: 419 us -> 281 us
  local copies, waits for them, and re-layouts: 79.5 us -> 62.7 us
  blocking collectives: 176 us -> 189 us
    ppermute x0 -> x8, waiting for transfers between devices: none -> 185 us  [raise_the_record(): lax.ppermute(high, along_axis, tuple(((tick, tick ^ even) for tick in ran...]
    all_gather x4, waiting for transfers between devices: 159 us -> 1.94 us  [gather_plane(): return lax.all_gather(rows, PLANE, axis=0, tiled=True)]
    all_gather x4 -> x0, waiting for transfers between devices: 153 us -> none  [gather_ctx(): return lax.all_gather(rows, 'ctx', axis=0, tiled=True)]
    all_to_all x0 -> x1, blocking collectives: none -> 11.3 us  [scatter_weight(): grad = lax.all_to_all(grad, 'ctx', 0, 0, tiled=True)]
    ppermute x0 -> x8, starting transfers between devices: none -> 8.94 us  [raise_the_record(): lax.ppermute(high, along_axis, tuple(((tick, tick ^ even) for tick in ran...]
    convert_element_type x1 -> x0, local copies, waits for them, and re-layouts: 8.75 us -> none  [scatter_weight(): grad = grad.astype(BF16).reshape(seqs, ctxs, cores, rows, grad.shape[1])]
    all_to_all x4 -> x3, waiting for transfers between devices: 52.7 us -> 45.4 us  [scatter_weight(): grad = lax.all_to_all(grad, 'ctx', 0, 0, tiled=True)]
  transfers between devices with their start and end apart: 18 -> 21, of which waited for: 13 -> 12; matrix products, arithmetic and copies ran while one was open for 21% -> 23% of each run, Pallas kernels for 0% -> 0%
where the time goes in v1:
time: 731 us; the launch traced here: 721 us
  waiting for transfers between devices  281 us (38%)
  blocking collectives  189 us (26%)
  matrix products  104 us (14%)
  local copies, waits for them, and re-layouts  62.7 us (9%)
  other arithmetic  37.2 us (5%)
  starting transfers between devices  31.2 us (4%)
  between operations  16.2 us (2%)
    ppermute x8, waiting for transfers between devices, raise_the_record(): lax.ppermute(high, along_axis, tuple(((tick, tick ^ even) for tick in ran...  185 us
    all_to_all x2, blocking collectives, scatter_ctx(): pieces = lax.all_to_all(partials.astype(BF16), 'ctx', 0, 0, tiled=True)  105 us
    all_to_all x3, waiting for transfers between devices, scatter_weight(): grad = lax.all_to_all(grad, 'ctx', 0, 0, tiled=True)  45.4 us
    all_to_all x1, waiting for transfers between devices, scatter_ctx(): pieces = lax.all_to_all(partials.astype(BF16), 'ctx', 0, 0, tiled=True)  40.5 us
    psum x1, blocking collectives, local(): lax.psum((attention_part, query_part, key_part, feedforward_part), ('seq'...  40.1 us
    dot_general x4, matrix products, rows_by(): return jnp.dot(left, right, preferred_element_type=F32)  36.8 us
    dot_general x4, matrix products, rows_by_t(): lax.dot_general(left, right, (((1,), (1,)), ((), ())), preferred_element_...  32 us
    dot_general x4, matrix products, t_by_rows(): lax.dot_general(left, right, (((0,), (0,)), ((), ())), preferred_element_...  19.8 us
  transfers between devices with their start and end apart: 21, of which 12 were waited for; matrix products, arithmetic and copies ran while one was open for 23% of the time, Pallas kernels for 0%

profile of v1, /device:TPU:0, one launch (start us, length us, event | category | flops | bytes accessed | tf_op | source)
XLA Modules:
  0.0 721.2 jit_solution(14190479509304898441)
XLA Ops:
  14.0 3.1 collective-permute-start
  19.5 14.3 %all-reduce = s32[8]{0:T(128)S(1)} all-reduce(s32[8]{0:T(128)S(1)} %bitcast_dynamic-update-slice_fusion), channel_id=2, replica_groups=mesh['seq'=4,'ctx'=4,'fsdp'=2] {'ctx'}, use_global_device_ids=true, to_apply=%add | all-reduce | flops 8 | bytes 64
  38.4 44.0 %collective-permute-done.1 = bf16[256,2048]{1,0:T(8,128)(2,1)S(1)} collective-permute-done((bf16[256,2048]{1,0:T(8,128)(2,1)S(1)}, bf16[256,2048]{1,0:T(8,128)(2,1)S(1)}, u32[]{:S(2)}, u32[]{:S(2)}) %collective-permute-start.1) | collective-permute-done | bytes 1048608 | tf_op jit(solution)/shard_map/ppermute | solution.py:24
  83.1 4.6 fusion.32
  97.0 17.6 %all_to_all.98 = bf16[4,128,512]{1,2,0:T(8,128)(2,1)} all-to-all(bf16[4,128,512]{1,2,0:T(8,128)(2,1)S(1)} %copy.195), channel_id=1, replica_groups=mesh['seq'=4,'ctx'=4,'fsdp'=2] {'ctx'}, dimensions={0} | all-to-all | bytes 1048576 | tf_op jit(solution)/shard_map/all_to_all | solution.py:203
  114.6 7.7 %multiply_reduce_fusion.5 = (f32[128]{0:T(128)S(1)}, f32[128,2048]{1,0:T(8,128)S(1)}) fusion(bf16[128,2048]{0,1:T(8,128)(2,1)} %bitcast.220, bf16[2048,2048]{1,0:T(8,128)(2,1)} %all-gather.8.cloned.1.call-done, bf16[1,128,2048]{2,1,0:T(8,128)(2,1)S(1)} %copy-done.5), kind=kOutput, calls=%fused_computation.86 | convolution fusion | flops 1074790272 | bytes 10486272 | tf_op jit(solution)/shard_map/dot_general | solution.py:73
  122.5 12.0 %collective-permute-done.2 = bf16[128,2048]{1,0:T(8,128)(2,1)S(1)} collective-permute-done((bf16[128,2048]{1,0:T(8,128)(2,1)S(1)}, bf16[128,2048]{1,0:T(8,128)(2,1)S(1)}, u32[]{:S(2)}, u32[]{:S(2)}) %collective-permute-start.2) | collective-permute-done | bytes 524320 | tf_op jit(solution)/shard_map/ppermute | solution.py:24
  137.0 30.6 %collective-permute-done.4 = bf16[128,2048]{1,0:T(8,128)(2,1)S(1)} collective-permute-done((bf16[128,2048]{1,0:T(8,128)(2,1)S(1)}, bf16[128,2048]{1,0:T(8,128)(2,1)S(1)}, u32[]{:S(2)}, u32[]{:S(2)}) %collective-permute-start.4) | collective-permute-done | bytes 524320 | tf_op jit(solution)/shard_map/ppermute | solution.py:24
  168.9 2.5 collective-permute-start.5
  171.4 32.1 %collective-permute-done.3 = bf16[256,2048]{1,0:T(8,128)(2,1)} collective-permute-done((bf16[256,2048]{1,0:T(8,128)(2,1)S(1)}, bf16[256,2048]{1,0:T(8,128)(2,1)}, u32[]{:S(2)}, u32[]{:S(2)}) %collective-permute-start.3) | collective-permute-done | bytes 1048608 | tf_op jit(solution)/shard_map/ppermute | solution.py:24
  203.5 14.3 %fusion.40 = f32[512,3072]{1,0:T(8,128)} fusion(bf16[2048,3072]{1,0:T(8,128)(2,1)} %all-gather.10.cloned.1.call-done, bf16[256,2048]{1,0:T(8,128)(2,1)} %collective-permute-done.3, bf16[256,2048]{1,0:T(8,128)(2,1)} %copy-done.31, pred[]{:T(512)S(6)} %eq.4), kind=kOutput, calls=%fused_computation.113 | convolution fusion | flops 6451888128 | bytes 20971520 | tf_op jit(solution)/shard_map/dot_general | solution.py:69
  217.8 7.9 %collective-permute-done.5 = bf16[256,2048]{1,0:T(8,128)(2,1)S(1)} collective-permute-done((bf16[256,2048]{1,0:T(8,128)(2,1)}, bf16[256,2048]{1,0:T(8,128)(2,1)S(1)}, u32[]{:S(2)}, u32[]{:S(2)}) %collective-permute-start.5) | collective-permute-done | bytes 1048608 | tf_op jit(solution)/shard_map/ppermute | solution.py:24
  227.6 12.0 %multiply_convert_fusion.1 = (bf16[512,1536]{1,0:T(8,128)(2,1)}, bf16[512,1536]{1,0:T(8,128)(2,1)}, bf16[512,1536]{1,0:T(8,128)(2,1)}) fusion(f32[512,3072]{1,0:T(8,128)} %fusion.40, bf16[2048,1536]{1,0:T(8,128)(2,1)} %all-gather.12.cloned.1.call-done, bf16[256,2048]{1,0:T(8,128)(2,1)S(1)} %collective-permute-done.5, ...), kind=kOutput, calls=%fused_computation.22 | convolution fusion | flops 3242459136 | bytes 19398656 | tf_op jit(solution)/shard_map/dot_general | solution.py:69
  239.6 8.7 %convolution_convert_fusion.3 = bf16[512,2048]{1,0:T(8,128)(2,1)S(1)} fusion(bf16[2048,3072]{1,0:T(8,128)(2,1)S(1)} %copy-done.44, bf16[512,1536]{1,0:T(8,128)(2,1)} %get-tuple-element.22, bf16[512,1536]{1,0:T(8,128)(2,1)} %get-tuple-element.21), kind=kOutput, calls=%fused_computation.26 | convolution fusion | flops 6449790976 | bytes 17825792 | tf_op jit(solution)/shard_map/dot_general | solution.py:73
  248.4 53.0 %all_to_all.99 = bf16[4,128,2048]{2,1,0:T(8,128)(2,1)S(1)} all-to-all(bf16[4,128,2048]{2,1,0:T(8,128)(2,1)S(1)} %bitcast.214), channel_id=1, replica_groups=mesh['seq'=4,'ctx'=4,'fsdp'=2] {'ctx'}, dimensions={0} | all-to-all | bytes 4194304 | tf_op jit(solution)/shard_map/all_to_all | solution.py:90
  303.1 12.7 %collective-permute-done.6 = bf16[128,2048]{1,0:T(8,128)(2,1)S(1)} collective-permute-done((bf16[128,2048]{1,0:T(8,128)(2,1)S(1)}, bf16[128,2048]{1,0:T(8,128)(2,1)S(1)}, u32[]{:S(2)}, u32[]{:S(2)}) %collective-permute-start.6) | collective-permute-done | bytes 524320 | tf_op jit(solution)/shard_map/ppermute | solution.py:24
  316.8 45.9 %collective-permute-done.7 = bf16[256,2048]{1,0:T(8,128)(2,1)S(1)} collective-permute-done((bf16[256,2048]{1,0:T(8,128)(2,1)S(1)}, bf16[256,2048]{1,0:T(8,128)(2,1)S(1)}, u32[]{:S(2)}, u32[]{:S(2)}) %collective-permute-start.7) | collective-permute-done | bytes 1048608 | tf_op jit(solution)/shard_map/ppermute | solution.py:24
  365.5 6.2 convolution_convert_fusion.1
  371.7 3.3 copy.223
  375.0 5.9 convolution_convert_fusion.6
  382.9 4.2 all-to-all-start.3
  392.0 2.5 copy.209
  394.6 7.5 %all-to-all-done.3 = bf16[128,4,512]{0,2,1:T(8,128)(2,1)} async-done(((bf16[128,4,512]{0,2,1:T(8,128)(2,1)}), bf16[128,4,512]{0,2,1:T(8,128)(2,1)}, u32[]{:S(2)}, u32[]{:S(2)}) %all-to-all-start.3) | async-done | bytes 524320 | tf_op jit(solution)/shard_map/all_to_all | solution.py:230
  406.4 4.5 fusion.18
  414.1 4.2 fusion.6
  423.1 3.5 broadcast_multiply_fusion.1
  426.6 2.5 copy.204
  432.7 2.7 copy.207
  435.4 2.3 copy.206
  440.6 2.6 copy.245
  449.0 3.1 convolution_convert_fusion.2
  452.0 2.4 copy.214
  455.6 9.2 %convolution_convert_fusion = bf16[2048,3072]{1,0:T(8,128)(2,1)S(1)} fusion(bf16[512,1536]{1,0:T(8,128)(2,1)} %get-tuple-element.22, bf16[512,1536]{1,0:T(8,128)(2,1)} %get-tuple-element.21, bf16[256,2048]{1,0:T(8,128)(2,1)} %collective-permute-done.3, bf16[256,2048]{1,0:T(8,128)(2,1)S(1)} %copy-done.32, pred[]{:T(512)S(6)} %eq.4), kind=kOutput, calls=%fused_computation | convolution fusion | flops 6464471040 | bytes 17825792 | tf_op jit(solution)/shard_map/dot_general | solution.py:77
  464.9 5.6 copy.220
  470.5 8.1 %convolution_convert_fusion.5 = bf16[512,2048]{1,0:T(8,128)(2,1)} fusion(bf16[512,1536]{1,0:T(8,128)(2,1)} %get-tuple-element.23, bf16[2048,1536]{1,0:T(8,128)(2,1)} %all-gather.12.cloned.1.call-done), kind=kOutput, calls=%fused_computation.28 | convolution fusion | flops 3222274048 | bytes 9961472 | tf_op jit(solution)/shard_map/dot_general | solution.py:73
  478.5 4.7 all-to-all-start.1
  483.2 7.6 %fusion.3 = (f32[2048]{0:T(1024)S(1)}, bf16[512,2048]{1,0:T(8,128)(2,1)}) fusion(f32[512]{0:T(512)S(1)} %add_rsqrt_fusion.2, bf16[256,2048]{1,0:T(8,128)(2,1)S(1)} %copy-done.19, bf16[256,2048]{1,0:T(8,128)(2,1)} %copy-done.34, pred[]{:T(512)S(6)} %eq.4, bf16[2048,1024]{1,0:T(8,128)(2,1)} %all-gather.6.cloned.1.call-done, ...), kind=kOutput, calls=%fused_computation.7 | convolution fusion | flops 2165307392 | bytes 9447425 | tf_op jit(solution)/shard_map/dot_general | solution.py:73
  490.8 40.5 %all-to-all-done.1 = bf16[4,128,2048]{2,1,0:T(8,128)(2,1)} async-done(((bf16[4,128,2048]{2,1,0:T(8,128)(2,1)}), bf16[4,128,2048]{2,1,0:T(8,128)(2,1)}, u32[]{:S(2)}, u32[]{:S(2)}) %all-to-all-start.1) | async-done | bytes 2097184 | tf_op jit(solution)/shard_map/all_to_all | solution.py:90
  531.3 52.3 %all_to_all.100 = bf16[4,128,2048]{2,1,0:T(8,128)(2,1)} all-to-all(bf16[4,128,2048]{2,1,0:T(8,128)(2,1)} %bitcast.212), channel_id=1, replica_groups=mesh['seq'=4,'ctx'=4,'fsdp'=2] {'ctx'}, dimensions={0} | all-to-all | bytes 4194304 | tf_op jit(solution)/shard_map/all_to_all | solution.py:90
  583.7 11.3 %all_to_all.101 = bf16[4,64,512]{2,1,0:T(8,128)(2,1)S(1)} all-to-all(bf16[4,64,512]{2,1,0:T(8,128)(2,1)} %bitcast.232), channel_id=1, replica_groups=mesh['seq'=4,'ctx'=4,'fsdp'=2] {'ctx'}, dimensions={0} | all-to-all | bytes 524288 | tf_op jit(solution)/shard_map/all_to_all | solution.py:101
  594.9 4.2 all-to-all-start.8
  599.3 18.0 %all-to-all-done.8 = bf16[4,64,1536]{2,1,0:T(8,128)(2,1)} async-done(((bf16[4,64,1536]{2,1,0:T(8,128)(2,1)}), bf16[4,64,1536]{2,1,0:T(8,128)(2,1)}, u32[]{:S(2)}, u32[]{:S(2)}) %all-to-all-start.8) | async-done | bytes 786464 | tf_op jit(solution)/shard_map/all_to_all | solution.py:101
  617.3 4.1 all-to-all-start.5
  621.5 3.0 convert_reduce_fusion.2
  624.5 40.1 %all-reduce.1 = (f32[2048]{0:T(1024)}, f32[128]{0:T(128)}, f32[128]{0:T(128)}, f32[2048]{0:T(1024)}) all-reduce(f32[2048]{0:T(1024)S(1)} %get-tuple-element.26, f32[128]{0:T(128)S(1)} %get-tuple-element.10, f32[128]{0:T(128)S(1)} %get-tuple-element.14, ...), channel_id=1, replica_groups=mesh['seq'=4,'ctx'=4,'fsdp'=2] {'seq','ctx','fsdp'}, use_global_device_ids=true, to_apply=%region_16.17 | all-reduce | flops 4352 | bytes 34816 | tf_op jit(solution)/shard_map/psum | solution.py:271
  668.1 4.4 all-to-all-start.7
  672.5 3.0 fusion.35
  682.0 27.4 %all-to-all-done.7 = bf16[4,64,3072]{2,1,0:T(8,128)(2,1)} async-done(((bf16[4,64,3072]{2,1,0:T(8,128)(2,1)}), bf16[4,64,3072]{2,1,0:T(8,128)(2,1)}, u32[]{:S(2)}, u32[]{:S(2)}) %all-to-all-start.7) | async-done | bytes 1572896 | tf_op jit(solution)/shard_map/all_to_all | solution.py:101
  (228 shorter events, 81.2 us)
Async XLA Ops:
  7.2 11.3 %copy-start = (bf16[256,6144]{1,0:T(8,128)(2,1)S(1)}, bf16[256,6144]{1,0:T(8,128)(2,1)}, u32[]{:S(2)}) copy-start(bf16[256,6144]{1,0:T(8,128)(2,1)} %param.20) | copy-start | bytes 9437188
  7.2 75.9 %all-gather.6.cloned.1.call-start = ((), (), s32[]{:S(2)}) async-start(), calls=%async_computation.13 | async-start | bytes 4718592 | tf_op jit(solution)/shard_map/all_gather | solution.py:85
  10.3 104.3 %all-gather.8.cloned.1.call-start = ((), (), s32[]{:S(2)}) async-start(), calls=%async_computation.14 | async-start | bytes 9437184 | tf_op jit(solution)/shard_map/all_gather | solution.py:85
  11.0 192.4 %all-gather.10.cloned.1.call-start = ((), (), s32[]{:S(2)}) async-start(), calls=%async_computation.15 | async-start | bytes 14155776 | tf_op jit(solution)/shard_map/all_gather | solution.py:85
  12.5 4.6 copy-start.47
  12.6 5.8 copy-start.46
  13.9 213.7 %all-gather.12.cloned.1.call-start = ((), (), s32[]{:S(2)}) async-start(), calls=%async_computation.16 | async-start | bytes 7077888 | tf_op jit(solution)/shard_map/all_gather | solution.py:85
  14.0 19.8 %collective-permute-start = (bf16[128,2048]{1,0:T(8,128)(2,1)}, bf16[128,2048]{1,0:T(8,128)(2,1)}, u32[]{:S(2)}, u32[]{:S(2)}) collective-permute-start(bf16[128,2048]{1,0:T(8,128)(2,1)} %bitcast.193), channel_id=1, source_target_pairs={{0,2},{2,0},{4,6},{6,4},{1,3},{3,1},{5,7},{7,5},{8,10},{10,8},{12,... | collective-permute-start | bytes 1572872 | tf_op jit(solution)/shard_map/ppermute | solution.py:24
  19.4 63.7 %copy-start.41 = (f32[2048]{0:T(1024)S(1)}, f32[2048]{0:T(1024)}, u32[]{:S(2)}) copy-start(f32[2048]{0:T(1024)} %param.13) | copy-start | bytes 24580
  19.4 564.3 %reduce-scatter.7.cloned.1.call-start = ((), (), s32[]{:S(2)}) async-start(), calls=%async_computation.18 | async-start | bytes 2359296 | tf_op jit(solution)/shard_map/reduce_scatter | solution.py:100
  36.0 51.7 %copy-start.17 = (bf16[256,2048]{1,0:T(8,128)(2,1)}, bf16[256,2048]{1,0:T(8,128)(2,1)S(1)}, u32[]{:S(2)}) copy-start(bf16[256,2048]{1,0:T(8,128)(2,1)S(1)} %maximum_select_fusion.5) | copy-start | bytes 3145732
  36.0 46.3 %collective-permute-start.1 = (bf16[256,2048]{1,0:T(8,128)(2,1)S(1)}, bf16[256,2048]{1,0:T(8,128)(2,1)S(1)}, u32[]{:S(2)}, u32[]{:S(2)}) collective-permute-start(bf16[256,2048]{1,0:T(8,128)(2,1)S(1)} %maximum_select_fusion.5), channel_id=1, source_target_pairs={{0,4},{2,6},{4,0},{6,2},{1,5},{3,7},{5,1},{7,3},{8,12},{10,14},{12... | collective-permute-start | bytes 3145736 | tf_op jit(solution)/shard_map/ppermute | solution.py:24
  82.3 5.4 copy-start.34
  94.3 2.4 copy-start.2
  96.8 25.4 %copy-start.29 = (bf16[2,128,2,512]{3,1,2,0:T(8,128)(2,1)}, bf16[2,128,2,512]{3,1,2,0:T(8,128)(2,1)S(1)}, u32[]{:S(2)}) copy-start(bf16[2,128,2,512]{3,1,2,0:T(8,128)(2,1)S(1)} %convolution_convert_fusion.7) | copy-start | bytes 1572868
  96.8 17.8 %copy-start.5 = (bf16[1,128,2048]{2,1,0:T(8,128)(2,1)S(1)}, bf16[1,128,2048]{2,1,0:T(8,128)(2,1)}, u32[]{:S(2)}) copy-start(bf16[1,128,2048]{2,1,0:T(8,128)(2,1)} %param.11) | copy-start | bytes 1572868
  114.6 7.7 %copy-start.40 = (f32[2048]{0:T(1024)S(1)}, f32[2048]{0:T(1024)}, u32[]{:S(2)}) copy-start(f32[2048]{0:T(1024)} %param.16) | copy-start | bytes 24580
  122.2 13.1 %copy-start.10 = (bf16[1,128,2048]{2,1,0:T(8,128)(2,1)S(1)}, bf16[1,128,2048]{2,1,0:T(8,128)(2,1)}, u32[]{:S(2)}) copy-start(bf16[1,128,2048]{2,1,0:T(8,128)(2,1)} %param.21) | copy-start | bytes 1572868
  122.4 12.1 %collective-permute-start.2 = (bf16[128,2048]{1,0:T(8,128)(2,1)S(1)}, bf16[128,2048]{1,0:T(8,128)(2,1)S(1)}, u32[]{:S(2)}, u32[]{:S(2)}) collective-permute-start(bf16[128,2048]{1,0:T(8,128)(2,1)S(1)} %multiply_convert_fusion.3), channel_id=1, source_target_pairs={{0,2},{2,0},{4,6},{6,4},{1,3},{3,1},{5,7},{7,5},{8,10},{10,8},{12,... | collective-permute-start | bytes 1572872 | tf_op jit(solution)/shard_map/ppermute | solution.py:24
  134.8 34.1 %copy-start.31 = (bf16[256,2048]{1,0:T(8,128)(2,1)}, bf16[256,2048]{1,0:T(8,128)(2,1)S(1)}, u32[]{:S(2)}) copy-start(bf16[256,2048]{1,0:T(8,128)(2,1)S(1)} %maximum_select_fusion.6) | copy-start | bytes 3145732
  134.8 68.6 %collective-permute-start.3 = (bf16[256,2048]{1,0:T(8,128)(2,1)S(1)}, bf16[256,2048]{1,0:T(8,128)(2,1)}, u32[]{:S(2)}, u32[]{:S(2)}) collective-permute-start(bf16[256,2048]{1,0:T(8,128)(2,1)S(1)} %maximum_select_fusion.6), channel_id=1, source_target_pairs={{0,4},{2,6},{4,0},{6,2},{1,5},{3,7},{5,1},{7,3},{8,12},{10,14},{12... | collective-permute-start | bytes 3145736 | tf_op jit(solution)/shard_map/ppermute | solution.py:24
  135.3 32.4 %collective-permute-start.4 = (bf16[128,2048]{1,0:T(8,128)(2,1)S(1)}, bf16[128,2048]{1,0:T(8,128)(2,1)S(1)}, u32[]{:S(2)}, u32[]{:S(2)}) collective-permute-start(bf16[128,2048]{1,0:T(8,128)(2,1)S(1)} %bitcast.200), channel_id=1, source_target_pairs={{0,2},{2,0},{4,6},{6,4},{1,3},{3,1},{5,7},{7,5},{8,10},{10,8},{12,... | collective-permute-start | bytes 1572872 | tf_op jit(solution)/shard_map/ppermute | solution.py:24
  168.9 56.8 %collective-permute-start.5 = (bf16[256,2048]{1,0:T(8,128)(2,1)}, bf16[256,2048]{1,0:T(8,128)(2,1)S(1)}, u32[]{:S(2)}, u32[]{:S(2)}) collective-permute-start(bf16[256,2048]{1,0:T(8,128)(2,1)} %maximum_select_fusion.7), channel_id=1, source_target_pairs={{0,4},{2,6},{4,0},{6,2},{1,5},{3,7},{5,1},{7,3},{8,12},{10,14},{12... | collective-permute-start | bytes 3145736 | tf_op jit(solution)/shard_map/ppermute | solution.py:24
  225.7 13.9 %copy-start.45 = (bf16[256,2048]{1,0:T(8,128)(2,1)}, bf16[256,2048]{1,0:T(8,128)(2,1)S(1)}, u32[]{:S(2)}) copy-start(bf16[256,2048]{1,0:T(8,128)(2,1)S(1)} %collective-permute-done.5) | copy-start | bytes 3145732
  227.6 12.0 %copy-start.44 = (bf16[2048,3072]{1,0:T(8,128)(2,1)S(1)}, bf16[2048,3072]{1,0:T(8,128)(2,1)}, u32[]{:S(2)}) copy-start(bf16[2048,3072]{1,0:T(8,128)(2,1)} %all-gather.10.cloned.1.call-done) | copy-start | bytes 37748740
  302.1 60.5 %copy-start.30 = (bf16[2,128,2,512]{3,1,2,0:T(8,128)(2,1)S(1)}, bf16[2,128,2,512]{3,1,2,0:T(8,128)(2,1)}, u32[]{:S(2)}) copy-start(bf16[2,128,2,512]{3,1,2,0:T(8,128)(2,1)} %copy-done.29) | copy-start | bytes 1572868
  302.8 13.0 %copy-start.9 = (bf16[128,2048]{1,0:T(8,128)(2,1)}, bf16[128,2048]{1,0:T(8,128)(2,1)S(1)}, u32[]{:S(2)}) copy-start(bf16[128,2048]{1,0:T(8,128)(2,1)S(1)} %fusion.56) | copy-start | bytes 1572868
  302.8 13.0 %collective-permute-start.6 = (bf16[128,2048]{1,0:T(8,128)(2,1)S(1)}, bf16[128,2048]{1,0:T(8,128)(2,1)S(1)}, u32[]{:S(2)}, u32[]{:S(2)}) collective-permute-start(bf16[128,2048]{1,0:T(8,128)(2,1)S(1)} %fusion.56), channel_id=1, source_target_pairs={{0,2},{2,0},{4,6},{6,4},{1,3},{3,1},{5,7},{7,5},{8,10},{10,8},{12,... | collective-permute-start | bytes 1572872 | tf_op jit(solution)/shard_map/ppermute | solution.py:24
  316.1 46.6 %collective-permute-start.7 = (bf16[256,2048]{1,0:T(8,128)(2,1)S(1)}, bf16[256,2048]{1,0:T(8,128)(2,1)S(1)}, u32[]{:S(2)}, u32[]{:S(2)}) collective-permute-start(bf16[256,2048]{1,0:T(8,128)(2,1)S(1)} %maximum_select_fusion.8), channel_id=1, source_target_pairs={{0,4},{2,6},{4,0},{6,2},{1,5},{3,7},{5,1},{7,3},{8,12},{10,14},{12... | collective-permute-start | bytes 3145736 | tf_op jit(solution)/shard_map/ppermute | solution.py:24
  365.5 229.5 %reduce-scatter.11.cloned.1.call-start = ((), (), s32[]{:S(2)}) async-start(), calls=%async_computation.20 | async-start | bytes 7077888 | tf_op jit(solution)/shard_map/reduce_scatter | solution.py:100
  382.9 19.2 %all-to-all-start.3 = ((bf16[128,4,512]{0,2,1:T(8,128)(2,1)}), bf16[128,4,512]{0,2,1:T(8,128)(2,1)}, u32[]{:S(2)}, u32[]{:S(2)}) async-start(bf16[128,4,512]{0,2,1:T(8,128)(2,1)} %bitcast.217), calls=%async_computation.3 | async-start | bytes 1048576 | tf_op jit(solution)/shard_map/all_to_all | solution.py:230
  387.1 212.2 %reduce-scatter.5.cloned.1.call-start = ((), (), s32[]{:S(2)}) async-start(), calls=%async_computation.17 | async-start | bytes 4718592 | tf_op jit(solution)/shard_map/reduce_scatter | solution.py:100
  414.1 4.3 copy-start.14
  414.1 4.3 copy-start.27
  440.6 6.5 copy-start.33
  443.2 4.1 copy-start.15
  443.2 4.1 copy-start.16
  443.2 4.1 copy-start.25
  449.0 3.1 copy-start.36
  454.4 213.6 %reduce-scatter.9.cloned.1.call-start = ((), (), s32[]{:S(2)}) async-start(), calls=%async_computation.19 | async-start | bytes 14155776 | tf_op jit(solution)/shard_map/reduce_scatter | solution.py:100
  478.5 4.7 copy-start.19
  478.5 52.8 %all-to-all-start.1 = ((bf16[4,128,2048]{2,1,0:T(8,128)(2,1)}), bf16[4,128,2048]{2,1,0:T(8,128)(2,1)}, u32[]{:S(2)}, u32[]{:S(2)}) async-start(bf16[4,128,2048]{2,1,0:T(8,128)(2,1)} %bitcast.211), calls=%async_computation.1 | async-start | bytes 4194304 | tf_op jit(solution)/shard_map/all_to_all | solution.py:90
  531.3 67.8 %copy-start.6 = (bf16[1,128,2048]{2,1,0:T(8,128)(2,1)S(1)}, bf16[1,128,2048]{2,1,0:T(8,128)(2,1)}, u32[]{:S(2)}) copy-start(bf16[1,128,2048]{2,1,0:T(8,128)(2,1)} %param.11) | copy-start | bytes 1572868
  594.9 22.4 %all-to-all-start.8 = ((bf16[4,64,1536]{2,1,0:T(8,128)(2,1)}), bf16[4,64,1536]{2,1,0:T(8,128)(2,1)}, u32[]{:S(2)}, u32[]{:S(2)}) async-start(bf16[4,64,1536]{2,1,0:T(8,128)(2,1)} %bitcast.225), calls=%async_computation.12 | async-start | bytes 1572864 | tf_op jit(solution)/shard_map/all_to_all | solution.py:101
  617.3 50.7 %all-to-all-start.5 = ((bf16[4,64,1024]{2,1,0:T(8,128)(2,1)}), bf16[4,64,1024]{2,1,0:T(8,128)(2,1)}, u32[]{:S(2)}, u32[]{:S(2)}) async-start(bf16[4,64,1024]{2,1,0:T(8,128)(2,1)} %bitcast.228), calls=%async_computation.6 | async-start | bytes 1048576 | tf_op jit(solution)/shard_map/all_to_all | solution.py:101
  667.7 4.7 copy-start.12
  668.1 41.3 %all-to-all-start.7 = ((bf16[4,64,3072]{2,1,0:T(8,128)(2,1)}), bf16[4,64,3072]{2,1,0:T(8,128)(2,1)}, u32[]{:S(2)}, u32[]{:S(2)}) async-start(bf16[4,64,3072]{2,1,0:T(8,128)(2,1)} %bitcast.221), calls=%async_computation.10 | async-start | bytes 3145728 | tf_op jit(solution)/shard_map/all_to_all | solution.py:101
  710.9 3.0 copy-start.1
  (21 other events, 28.6 us)
Sparse Core Ops, SparseCore 0:
  10.5 39.2 all-gather.5
  51.7 54.2 all-gather.7
  108.5 71.9 all-gather.9
  182.2 45.3 all-gather.11
  365.6 39.9 reduce-scatter.6
  408.8 61.7 reduce-scatter.10
  473.9 51.1 reduce-scatter.4
  528.6 92.2 reduce-scatter.8
